TPU v7x, 32 devices: a whole 2x2x4 slice. The times are simulated.
32 devices in a mesh: dp: 4 (over y, x), ctx: 4 (over z), tp: 2 (over core).
Axes of the slice: x: 2, y: 2, z: 4, core: 2. Of those that a mesh axis runs over, the one named last changes fastest.
Arguments:
- tokens: bfloat16 [8, 2048, 768], P('dp', 'ctx'), may hold values from -6 to 6
- segments: int32 [8, 2048], P('dp', 'ctx'), may hold values from 0 to 7, never falling along the last dimension, each value on 1 to 768 neighbouring positions
- cotangent: bfloat16 [8, 2048, 768], P('dp', 'ctx'), may hold values from -6 to 6
- w_qkv: bfloat16 [768, 3, 768], P('dp', None, 'tp'), may hold values from -0.21875 to 0.21875
- w_out: bfloat16 [768, 768], P('dp', 'tp'), may hold values from -1.75 to 1.75
- w_gate: bfloat16 [768, 3072], P('dp', 'tp'), may hold values from -0.21875 to 0.21875
- w_up: bfloat16 [768, 3072], P('dp', 'tp'), may hold values from -0.21875 to 0.21875
- w_down: bfloat16 [768, 3072], P('dp', 'tp'), may hold values from -0.109375 to 0.109375
- norm_gain: bfloat16 [768], P('dp'), may hold values from 0.5 to 1.5
- norm_bias: bfloat16 [768], P('dp'), may hold values from -3 to 3
- final_gain: bfloat16 [768], P('dp'), may hold values from 0.5 to 1.5
- final_bias: bfloat16 [768], P('dp'), may hold values from -3 to 3
Outputs:
- output: bfloat16 [8, 2048, 768], P('dp', 'ctx')
- d_tokens: bfloat16 [8, 2048, 768], P('dp', 'ctx')
- d_qkv: float32 [768, 3, 768], P('dp', None, 'tp')
- d_out: float32 [768, 768], P('dp', 'tp')
- d_gate: float32 [768, 3072], P('dp', 'tp')
- d_up: float32 [768, 3072], P('dp', 'tp')
- d_down: float32 [768, 3072], P('dp', 'tp')
- d_norm_gain: float32 [768], P('dp')
- d_norm_bias: float32 [768], P('dp')
- d_final_gain: float32 [768], P('dp')
- d_final_bias: float32 [768], P('dp')
Inputs may be any that keep to these rules, and one draw needn't show every extreme that they name: `segments`: within each sequence the segment numbers never fall, and each document is a run of consecutive tokens.
All inputs are finite; a program needn't handle non-finite values.
Results may differ from a plain program's by a relative error of at most 0.023.
Values may be sent and summed in bfloat16 or wider, within the bound.
No kernel may reach another device: no remote copies, remote signals or barrier semaphores. Data moves between devices by JAX's collectives and lax.ppermute only.
A program may use at most 192 MiB of HBM per device.

v0:
```python
import jax
import jax.numpy as jnp
from jax import lax
from jax.sharding import PartitionSpec as P

HD = 64
epsilon = 1e-12
rotary_base = 1000.0


def rotary_tables(offset, length, head_size):
    half_size = head_size // 2
    places = (offset + jnp.arange(length)).astype(jnp.float32)
    inverse = rotary_base ** (-(jnp.arange(half_size).astype(jnp.float32) * 2.0 / head_size))
    angles = places[:, None] * inverse[None, :]
    angles = jnp.concatenate([angles, angles], axis=1)
    return (jnp.cos(angles), jnp.sin(angles))


def rotate_pairs(vector, cosine, sine_t):
    half_size = vector.shape[-1] // 2
    turned = jnp.concatenate([-vector[..., half_size:], vector[..., :half_size]], axis=-1)
    return vector * cosine[:, None, :] + turned * sine_t[:, None, :]


def rotate_back(gradient, cosine, sine_t):
    half_size = gradient.shape[-1] // 2
    moved = gradient * sine_t[:, None, :]
    turned = jnp.concatenate([moved[..., half_size:], -moved[..., :half_size]], axis=-1)
    return gradient * cosine[:, None, :] + turned


def norm_forward(values, gain_v, bias_v):
    average = jnp.mean(values, -1, keepdims=True)
    centred = values - average
    inv_std = lax.rsqrt(jnp.mean(centred * centred, -1, keepdims=True) + epsilon)
    unit_v = centred * inv_std
    return (unit_v * gain_v + bias_v, unit_v, inv_std)


def norm_backward(gradient, unit_v, inv_std, gain_v):
    scaled = gradient * gain_v
    dvalues = (
        scaled
        - jnp.mean(scaled, -1, keepdims=True)
        - unit_v * jnp.mean(scaled * unit_v, -1, keepdims=True)
    ) * inv_std
    return (dvalues, jnp.sum(gradient * unit_v, 0), jnp.sum(gradient, 0))


def contract_rows(left, right):
    return lax.dot_general(
        left, right, (((0,), (0,)), ((), ())), preferred_element_type=jnp.float32
    )


def contract_cols(left, right):
    return lax.dot_general(
        left, right, (((1,), (1,)), ((), ())), preferred_element_type=jnp.float32
    )


def masked_scores(queries, keys_rot, seg_query, seg_key, factor):
    raw = jnp.einsum("qhd,khd->hqk", queries, keys_rot, preferred_element_type=jnp.float32) * factor
    same_doc = seg_query[:, None] == seg_key[None, :]
    return jnp.where(same_doc[None], raw, -1e30)


def body(
    tokens,
    segments,
    cotangent,
    w_qkv,
    w_out,
    w_gate,
    w_up,
    w_down,
    norm_gain,
    norm_bias,
    final_gain,
    final_bias,
):
    seq_count, row_count, model_width = tokens.shape
    tok_count = seq_count * row_count
    factor = HD ** (-0.5)
    gathered = (
        lax.all_gather(w_qkv, "dp", axis=0, tiled=True),
        lax.all_gather(w_out, "dp", axis=0, tiled=True),
        lax.all_gather(w_gate, "dp", axis=0, tiled=True),
        lax.all_gather(w_up, "dp", axis=0, tiled=True),
        lax.all_gather(w_down, "dp", axis=0, tiled=True),
        lax.all_gather(norm_gain, "dp", axis=0, tiled=True),
        lax.all_gather(norm_bias, "dp", axis=0, tiled=True),
        lax.all_gather(final_gain, "dp", axis=0, tiled=True),
        lax.all_gather(final_bias, "dp", axis=0, tiled=True),
    )
    qkv_w, out_w, gate_w, up_w, down_w = (
        gathered[0],
        gathered[1],
        gathered[2],
        gathered[3],
        gathered[4],
    )
    gain_one = gathered[5].astype(jnp.float32)
    bias_one = gathered[6].astype(jnp.float32)
    gain_two = gathered[7].astype(jnp.float32)
    bias_two = gathered[8].astype(jnp.float32)
    local_width = qkv_w.shape[2]
    head_count = local_width // HD
    flat_in = tokens.reshape(tok_count, model_width)
    mixed_qkv = jnp.einsum("td,dcn->tcn", flat_in, qkv_w, preferred_element_type=jnp.float32)
    cosine, sine_t = rotary_tables(lax.axis_index("ctx") * row_count, row_count, HD)
    pieces = mixed_qkv.reshape(seq_count, row_count, 3, head_count, HD)
    queries = rotate_pairs(pieces[:, :, 0], cosine, sine_t).astype(jnp.bfloat16)
    keys_rot = (
        rotate_pairs(pieces[:, :, 1], cosine, sine_t)
        .astype(jnp.bfloat16)
        .reshape(seq_count, row_count, local_width)
    )
    valued = pieces[:, :, 2].astype(jnp.bfloat16).reshape(seq_count, row_count, local_width)
    all_keys, all_values = (
        lax.all_gather(keys_rot, "ctx", axis=1, tiled=True),
        lax.all_gather(valued, "ctx", axis=1, tiled=True),
    )
    all_docs = lax.all_gather(segments, "ctx", axis=1, tiled=True)
    length = all_keys.shape[1]
    key_heads = all_keys.reshape(seq_count, length, head_count, HD)
    value_heads = all_values.reshape(seq_count, length, head_count, HD)

    def attend(blocks):
        query_blk, key_blk, value_blk, seg_query, seg_key = blocks
        scores = masked_scores(query_blk, key_blk, seg_query, seg_key, factor)
        largest = jnp.max(scores, -1, keepdims=True)
        exp_scores = jnp.exp(scores - largest)
        row_total = jnp.sum(exp_scores, -1, keepdims=True)
        chances = (exp_scores / row_total).astype(jnp.bfloat16)
        mixture = jnp.einsum("hqk,khd->qhd", chances, value_blk, preferred_element_type=jnp.float32)
        return (mixture.astype(jnp.bfloat16), (largest + jnp.log(row_total))[..., 0])

    mixture, log_total = lax.map(attend, (queries, key_heads, value_heads, segments, all_docs))
    mixture_flat = mixture.reshape(tok_count, local_width)
    attended = lax.psum(contract_cols(mixture_flat, out_w).astype(jnp.bfloat16), "tp").astype(
        jnp.float32
    )
    normed, unit_one, inv_one = norm_forward(
        flat_in.astype(jnp.float32) + attended, gain_one, bias_one
    )
    normed_low = normed.astype(jnp.bfloat16)
    gate_pre = jnp.dot(normed_low, gate_w, preferred_element_type=jnp.float32)
    up_pre = jnp.dot(normed_low, up_w, preferred_element_type=jnp.float32)
    sigmoid_g = jax.nn.sigmoid(gate_pre)
    activated = gate_pre * sigmoid_g
    hidden_low = (activated * up_pre).astype(jnp.bfloat16)
    branch = lax.psum(contract_cols(hidden_low, down_w).astype(jnp.bfloat16), "tp").astype(
        jnp.float32
    )
    final_out, unit_two, inv_two = norm_forward(normed + branch, gain_two, bias_two)
    output = final_out.astype(jnp.bfloat16).reshape(seq_count, row_count, model_width)
    back_weights = (
        lax.all_gather(w_qkv, "dp", axis=0, tiled=True),
        lax.all_gather(w_out, "dp", axis=0, tiled=True),
        lax.all_gather(w_gate, "dp", axis=0, tiled=True),
        lax.all_gather(w_up, "dp", axis=0, tiled=True),
        lax.all_gather(w_down, "dp", axis=0, tiled=True),
        lax.all_gather(norm_gain, "dp", axis=0, tiled=True),
        lax.all_gather(norm_bias, "dp", axis=0, tiled=True),
        lax.all_gather(final_gain, "dp", axis=0, tiled=True),
        lax.all_gather(final_bias, "dp", axis=0, tiled=True),
    )
    qkv_b, out_b, gate_b, up_b, down_b = (
        back_weights[0],
        back_weights[1],
        back_weights[2],
        back_weights[3],
        back_weights[4],
    )
    gain_one_b = back_weights[5].astype(jnp.float32)
    gain_two_b = back_weights[7].astype(jnp.float32)
    grad_out = cotangent.reshape(tok_count, model_width).astype(jnp.float32)
    dsum, dgain_two, dbias_two = norm_backward(grad_out, unit_two, inv_two, gain_two_b)
    dbranch = dsum.astype(jnp.bfloat16)
    d_down = contract_rows(dbranch, hidden_low)
    dhidden = jnp.dot(dbranch, down_b, preferred_element_type=jnp.float32)
    dgate = (dhidden * up_pre * sigmoid_g * (1.0 + gate_pre * (1.0 - sigmoid_g))).astype(
        jnp.bfloat16
    )
    dup = (dhidden * activated).astype(jnp.bfloat16)
    d_gate = contract_rows(normed_low, dgate)
    d_up = contract_rows(normed_low, dup)
    dnormed_part = contract_cols(dgate, gate_b) + contract_cols(dup, up_b)
    dnormed = dsum + lax.psum(dnormed_part.astype(jnp.bfloat16), "tp").astype(jnp.float32)
    dresid, dgain_one, dbias_one = norm_backward(dnormed, unit_one, inv_one, gain_one_b)
    dattended = dresid.astype(jnp.bfloat16)
    d_out = contract_rows(dattended, mixture_flat)
    dmixture = jnp.dot(dattended, out_b, preferred_element_type=jnp.float32).astype(jnp.bfloat16)
    dmixture = dmixture.reshape(seq_count, row_count, head_count, HD)

    def attend_back(blocks):
        query_blk, key_blk, value_blk, seg_query, seg_key, log_blk, dmix_blk = blocks
        scores = masked_scores(query_blk, key_blk, seg_query, seg_key, factor)
        chances = jnp.exp(scores - log_blk[..., None])
        dchances = jnp.einsum(
            "qhd,khd->hqk", dmix_blk, value_blk, preferred_element_type=jnp.float32
        )
        row_dot = jnp.sum(chances * dchances, -1, keepdims=True)
        dscores = (chances * (dchances - row_dot)).astype(jnp.bfloat16)
        dquery = (
            jnp.einsum("hqk,khd->qhd", dscores, key_blk, preferred_element_type=jnp.float32)
            * factor
        )
        dkey = (
            jnp.einsum("hqk,qhd->khd", dscores, query_blk, preferred_element_type=jnp.float32)
            * factor
        )
        dvalue = jnp.einsum(
            "hqk,qhd->khd",
            chances.astype(jnp.bfloat16),
            dmix_blk,
            preferred_element_type=jnp.float32,
        )
        return (dquery, dkey.reshape(dkey.shape[0], -1), dvalue.reshape(dvalue.shape[0], -1))

    dqueries, dkeys_all, dvalues_all = lax.map(
        attend_back, (queries, key_heads, value_heads, segments, all_docs, log_total, dmixture)
    )
    dkeys_own, dvalues_own = (
        lax.psum_scatter(
            dkeys_all.astype(jnp.bfloat16), "ctx", scatter_dimension=1, tiled=True
        ).astype(jnp.float32),
        lax.psum_scatter(
            dvalues_all.astype(jnp.bfloat16), "ctx", scatter_dimension=1, tiled=True
        ).astype(jnp.float32),
    )
    dkey_heads = dkeys_own.reshape(seq_count, row_count, head_count, HD)
    dvalue_heads = dvalues_own.reshape(seq_count, row_count, head_count, HD)
    dquery_raw = rotate_back(dqueries, cosine, sine_t)
    dkey_raw = rotate_back(dkey_heads, cosine, sine_t)
    dqkv = (
        jnp.stack([dquery_raw, dkey_raw, dvalue_heads], 2)
        .reshape(tok_count, 3, local_width)
        .astype(jnp.bfloat16)
    )
    dinput_part = jnp.einsum("tcn,dcn->td", dqkv, qkv_b, preferred_element_type=jnp.float32)
    dinput = dresid + lax.psum(dinput_part.astype(jnp.bfloat16), "tp").astype(jnp.float32)
    d_tokens = dinput.astype(jnp.bfloat16).reshape(seq_count, row_count, model_width)
    d_qkv = jnp.einsum("td,tcn->dcn", flat_in, dqkv, preferred_element_type=jnp.float32)
    grad_terms = (d_qkv, d_out, d_gate, d_up, d_down, dgain_one, dbias_one, dgain_two, dbias_two)
    group_part = (
        lax.psum_scatter(
            grad_terms[0].astype(jnp.bfloat16), "dp", scatter_dimension=0, tiled=True
        ).astype(jnp.float32),
        lax.psum_scatter(
            grad_terms[1].astype(jnp.bfloat16), "dp", scatter_dimension=0, tiled=True
        ).astype(jnp.float32),
        lax.psum_scatter(
            grad_terms[2].astype(jnp.bfloat16), "dp", scatter_dimension=0, tiled=True
        ).astype(jnp.float32),
        lax.psum_scatter(
            grad_terms[3].astype(jnp.bfloat16), "dp", scatter_dimension=0, tiled=True
        ).astype(jnp.float32),
        lax.psum_scatter(
            grad_terms[4].astype(jnp.bfloat16), "dp", scatter_dimension=0, tiled=True
        ).astype(jnp.float32),
        lax.psum_scatter(
            grad_terms[5].astype(jnp.bfloat16), "dp", scatter_dimension=0, tiled=True
        ).astype(jnp.float32),
        lax.psum_scatter(
            grad_terms[6].astype(jnp.bfloat16), "dp", scatter_dimension=0, tiled=True
        ).astype(jnp.float32),
        lax.psum_scatter(
            grad_terms[7].astype(jnp.bfloat16), "dp", scatter_dimension=0, tiled=True
        ).astype(jnp.float32),
        lax.psum_scatter(
            grad_terms[8].astype(jnp.bfloat16), "dp", scatter_dimension=0, tiled=True
        ).astype(jnp.float32),
    )
    reduced = (
        lax.psum(group_part[0].astype(jnp.bfloat16), "ctx").astype(jnp.float32),
        lax.psum(group_part[1].astype(jnp.bfloat16), "ctx").astype(jnp.float32),
        lax.psum(group_part[2].astype(jnp.bfloat16), "ctx").astype(jnp.float32),
        lax.psum(group_part[3].astype(jnp.bfloat16), "ctx").astype(jnp.float32),
        lax.psum(group_part[4].astype(jnp.bfloat16), "ctx").astype(jnp.float32),
        lax.psum(group_part[5].astype(jnp.bfloat16), "ctx").astype(jnp.float32),
        lax.psum(group_part[6].astype(jnp.bfloat16), "ctx").astype(jnp.float32),
        lax.psum(group_part[7].astype(jnp.bfloat16), "ctx").astype(jnp.float32),
        lax.psum(group_part[8].astype(jnp.bfloat16), "ctx").astype(jnp.float32),
    )
    return (output, d_tokens) + tuple(reduced)


def solution(mesh):
    placed = (
        P("dp", "ctx", None),
        P("dp", "ctx"),
        P("dp", "ctx", None),
        P("dp", None, "tp"),
        P("dp", "tp"),
        P("dp", "tp"),
        P("dp", "tp"),
        P("dp", "tp"),
        P("dp"),
        P("dp"),
        P("dp"),
        P("dp"),
    )
    return jax.shard_map(
        body,
        mesh=mesh,
        in_specs=placed,
        out_specs=(
            P("dp", "ctx", None),
            P("dp", "ctx", None),
            P("dp", None, "tp"),
            P("dp", "tp"),
            P("dp", "tp"),
            P("dp", "tp"),
            P("dp", "tp"),
            P("dp"),
            P("dp"),
            P("dp"),
            P("dp"),
        ),
        check_vma=False,
    )
```

profile of v0, /device:TPU:0, one launch (start us, length us, event | category | flops | bytes accessed | tf_op | source)
XLA Modules:
  0.0 1096.9 jit_solution(12073563558076399821)
XLA Ops:
  8.0 37.1 %all-gather.7.cloned.1.call-done = bf16[768,3,384]{2,0,1:T(8,128)(2,1)} async-done(((bf16[192,3,384]{2,0,1:T(8,128)(2,1)}), bf16[768,3,384]{2,0,1:T(8,128)(2,1)}) %all-gather.7.cloned.1.call-update) | async-done | bytes 1769488 | tf_op jit(solution)/shard_map/all_gather | solution.py:87
  57.8 13.6 %all_gather.45 = s32[2,2048]{1,0:T(2,128)S(1)} all-gather(s32[2,512]{1,0:T(2,128)S(1)} %copy-done.34), channel_id=1, replica_groups=mesh['dp'=4,'ctx'=4,'tp'=2] {'ctx'}, dimensions={1}, use_global_device_ids=true | all-gather | bytes 20480 | tf_op jit(solution)/shard_map/all_gather | solution.py:125
  71.4 11.4 %all_gather.47 = bf16[768,384]{1,0:T(8,128)(2,1)} all-gather(bf16[192,384]{1,0:T(8,128)(2,1)S(1)} %copy-done.35), channel_id=1, replica_groups=mesh['dp'=4,'ctx'=4,'tp'=2] {'dp'}, dimensions={0}, use_global_device_ids=true | all-gather | bytes 737280 | tf_op jit(solution)/shard_map/all_gather | solution.py:88
  84.9 31.7 %all-gather.9.cloned.1.call-done = bf16[2,2048,384]{1,2,0:T(8,128)(2,1)} async-done(((bf16[2,512,384]{1,2,0:T(8,128)(2,1)}), bf16[2,2048,384]{1,2,0:T(8,128)(2,1)}) %all-gather.9.cloned.1.call-update) | async-done | bytes 3145744 | tf_op jit(solution)/shard_map/all_gather | solution.py:123
  116.6 64.3 %all-gather.11.cloned.1.call-done = bf16[2,2048,384]{1,2,0:T(8,128)(2,1)} async-done(((bf16[2,512,384]{1,2,0:T(8,128)(2,1)}), bf16[2,2048,384]{1,2,0:T(8,128)(2,1)}) %all-gather.11.cloned.1.call-update) | async-done | bytes 3145744 | tf_op jit(solution)/shard_map/all_gather | solution.py:122
  180.9 73.4 %while.26 = (s32[]{:T(128)}, bf16[2,512,6,64]{1,3,2,0:T(8,128)(2,1)S(1)}, f32[2,6,512]{2,1,0:T(8,128)S(1)}, bf16[2,2048,6,64]{1,3,2,0:T(8,128)(2,1)}, s32[2,512]...) while((s32[]{:T(128)}, ...), condition=%wide.region_3.4_spmd, body=%wide.region_0.3_spmd.sunk | while | flops 1687352320 | bytes 96358544 | solution.py:140
  181.6 12.2 %fusion.139 = (f32[6,512]{1,0:T(8,128)S(1)}, f32[6,512,2048]{2,1,0:T(8,128)}) fusion(pred[512,2048]{1,0:T(8,128)(4,1)S(1)} %broadcast_compare_fusion.4, bf16[2,2048,6,64]{1,3,2,0:T(8,128)(2,1)} %get-tuple-element.429, s32[]{:T(128)S(6)} %copy.77, bf16[2,512,6,64]{1,3,2,0:T(8,128)(2,1)S(1)} %get-tuple-element.428), kind=kOutput, calls=%fused_computation.3.clone.1 | convolution fusion | flops 824177664 | bytes 28193792 | tf_op jit(solution)/shard_map/while/body/eval_jaxpr/qhd,khd->hqk/dot_general | solution.py:64
  193.8 12.1 %fusion.140 = f32[6,512]{1,0:T(8,128)S(1)} fusion(f32[6,512,2048]{2,1,0:T(8,128)} %get-tuple-element.387, f32[6,512]{1,0:T(8,128)S(1)} %get-tuple-element.388, pred[512,2048]{1,0:T(8,128)(4,1)S(1)} %broadcast_compare_fusion.4), kind=kLoop, calls=%fused_computation.4.clone.1 | loop fusion | flops 25162752 | bytes 26238976 | tf_op jit(solution)/shard_map/while/body/eval_jaxpr/reduce_sum | solution.py:135
  205.9 11.7 %fusion.141 = bf16[2,512,6,64]{1,3,2,0:T(8,128)(2,1)S(1)} fusion(bf16[2,512,6,64]{1,3,2,0:T(8,128)(2,1)S(1)} %get-tuple-element.414, s32[]{:T(128)S(6)} %copy.77, f32[6,512,2048]{2,1,0:T(8,128)} %get-tuple-element.387, f32[6,512]{1,0:T(8,128)S(1)} %fusion.140, f32[6,512]{1,0:T(8,128)S(1)} %get-tuple-element.388, ...), kind=kOutput, calls=%fused_computation.14.clone.1 | convolution fusion | flops 836960256 | bytes 28214272 | tf_op jit(solution)/shard_map/while/body/eval_jaxpr/hqk,khd->qhd/dot_general | solution.py:137
  218.3 12.2 %fusion.139 = (f32[6,512]{1,0:T(8,128)S(1)}, f32[6,512,2048]{2,1,0:T(8,128)}) fusion(pred[512,2048]{1,0:T(8,128)(4,1)S(1)} %broadcast_compare_fusion.4, bf16[2,2048,6,64]{1,3,2,0:T(8,128)(2,1)} %get-tuple-element.429, s32[]{:T(128)S(6)} %copy.77, bf16[2,512,6,64]{1,3,2,0:T(8,128)(2,1)S(1)} %get-tuple-element.428), kind=kOutput, calls=%fused_computation.3.clone.1 | convolution fusion | flops 824177664 | bytes 28193792 | tf_op jit(solution)/shard_map/while/body/eval_jaxpr/qhd,khd->hqk/dot_general | solution.py:64
  230.5 12.1 %fusion.140 = f32[6,512]{1,0:T(8,128)S(1)} fusion(f32[6,512,2048]{2,1,0:T(8,128)} %get-tuple-element.387, f32[6,512]{1,0:T(8,128)S(1)} %get-tuple-element.388, pred[512,2048]{1,0:T(8,128)(4,1)S(1)} %broadcast_compare_fusion.4), kind=kLoop, calls=%fused_computation.4.clone.1 | loop fusion | flops 25162752 | bytes 26238976 | tf_op jit(solution)/shard_map/while/body/eval_jaxpr/reduce_sum | solution.py:135
  242.6 11.7 %fusion.141 = bf16[2,512,6,64]{1,3,2,0:T(8,128)(2,1)S(1)} fusion(bf16[2,512,6,64]{1,3,2,0:T(8,128)(2,1)S(1)} %get-tuple-element.414, s32[]{:T(128)S(6)} %copy.77, f32[6,512,2048]{2,1,0:T(8,128)} %get-tuple-element.387, f32[6,512]{1,0:T(8,128)S(1)} %fusion.140, f32[6,512]{1,0:T(8,128)S(1)} %get-tuple-element.388, ...), kind=kOutput, calls=%fused_computation.14.clone.1 | convolution fusion | flops 836960256 | bytes 28214272 | tf_op jit(solution)/shard_map/while/body/eval_jaxpr/hqk,khd->qhd/dot_general | solution.py:137
  262.3 10.3 all-reduce.11
  282.3 35.4 %all-gather.13.cloned.1.call-done = bf16[768,1536]{1,0:T(8,128)(2,1)} async-done(((bf16[192,1536]{1,0:T(8,128)(2,1)}), bf16[768,1536]{1,0:T(8,128)(2,1)}) %all-gather.13.cloned.1.call-update) | async-done | bytes 2359312 | tf_op jit(solution)/shard_map/all_gather | solution.py:89
  317.7 7.4 fusion.96
  325.2 31.7 %all-gather.15.cloned.1.call-done = bf16[768,1536]{1,0:T(8,128)(2,1)} async-done(((bf16[192,1536]{1,0:T(8,128)(2,1)}), bf16[768,1536]{1,0:T(8,128)(2,1)}) %all-gather.15.cloned.1.call-update) | async-done | bytes 2359312 | tf_op jit(solution)/shard_map/all_gather | solution.py:90
  356.8 10.6 multiply_convert_fusion.3
  367.4 28.6 %all-gather.17.cloned.1.call-done = bf16[768,1536]{1,0:T(8,128)(2,1)} async-done(((bf16[192,1536]{1,0:T(8,128)(2,1)}), bf16[768,1536]{1,0:T(8,128)(2,1)}) %all-gather.17.cloned.1.call-update) | async-done | bytes 2359312 | tf_op jit(solution)/shard_map/all_gather | solution.py:91
  396.0 6.4 convolution_convert_fusion.5
  404.8 18.2 %all-reduce.20.cloned.1.call-done = bf16[1024,768]{1,0:T(8,128)(2,1)} async-done(((bf16[1024,768]{1,0:T(8,128)(2,1)}), bf16[1024,768]{1,0:T(8,128)(2,1)}) %all-reduce.20.cloned.1.call-update) | async-done | bytes 1572880 | tf_op jit(solution)/shard_map/psum | solution.py:154
  432.1 6.9 multiply_convert_fusion.1
  446.3 21.6 %all-reduce.22.cloned.1.call-done = bf16[1024,768]{1,0:T(8,128)(2,1)} async-done(((bf16[1024,768]{1,0:T(8,128)(2,1)}), bf16[1024,768]{1,0:T(8,128)(2,1)}) %all-reduce.22.cloned.1.call-update) | async-done | bytes 1572880 | tf_op jit(solution)/shard_map/psum | solution.py:191
  467.9 5.3 multiply_reduce_fusion.1
  478.5 156.4 %while.27 = (s32[]{:T(128)}, f32[2,512,6,64]{1,3,2,0:T(8,128)}, bf16[2,2048,384]{1,2,0:T(8,128)(2,1)}, bf16[2,2048,384]{1,2,0:T(8,128)(2,1)}, bf16[2,2048,6,64]{...) while((s32[]{:T(128)}, f32[2,512,6,64]{1,3,2,0:T(8,128)}, ...), condition=%wide.region_17.18_spmd, body=%wide.region_15.17_spmd.sunk | while | flops 4123718656 | bytes 226358576 | solution.py:223
  479.5 11.9 %fusion.150 = f32[6,512,2048]{2,1,0:T(8,128)} fusion(bf16[2,2048,6,64]{1,3,2,0:T(8,128)(2,1)} %get-tuple-element.459, s32[]{:T(128)S(6)} %copy.91, bf16[2,512,6,64]{1,3,2,0:T(8,128)(2,1)S(1)} %get-tuple-element.462), kind=kOutput, calls=%fused_computation.36.clone.1 | convolution fusion | flops 805306368 | bytes 27132928 | tf_op jit(solution)/shard_map/while/body/eval_jaxpr/qhd,khd->hqk/dot_general | solution.py:64
  491.4 12.8 %fusion.152 = bf16[6,64,2048]{2,1,0:T(8,128)(2,1)} fusion(f32[6,512,2048]{2,1,0:T(8,128)} %fusion.150, f32[6,512]{1,0:T(8,128)S(1)} %dynamic-slice_bitcast_fusion.2, pred[512,2048]{1,0:T(8,128)(4,1)S(1)} %broadcast_compare_fusion.5, bf16[2,512,6,64]{1,3,2,0:T(8,128)(2,1)S(1)} %get-tuple-element.464, s32[]{:T(128)S(6)} %copy.91), kind=kOutput, calls=%fused_computation.28.clone.1 | convolution fusion | flops 830472192 | bytes 28196868 | tf_op jit(solution)/shard_map/while/body/eval_jaxpr/hqk,qhd->khd/dot_general | solution.py:215
  504.2 20.0 %multiply_reduce_fusion.7 = (f32[6,512]{1,0:T(8,128)S(1)}, f32[6,512,2048]{2,1,0:T(8,128)}) fusion(f32[6,512,2048]{2,1,0:T(8,128)} %fusion.150, f32[6,512]{1,0:T(8,128)S(1)} %dynamic-slice_bitcast_fusion.2, pred[512,2048]{1,0:T(8,128)(4,1)S(1)} %broadcast_compare_fusion.5, bf16[2,2048,6,64]{1,3,2,0:T(8,128)(2,1)} %get-tuple-element.465, ...), kind=kOutput, calls=%fused_computation.25.clone.1 | convolution fusion | flops 836760576 | bytes 53376000 | tf_op jit(solution)/shard_map/while/body/eval_jaxpr/qhd,khd->hqk/dot_general | solution.py:202
  524.2 17.7 %multiply_convert_fusion.5 = bf16[6,512,2048]{2,1,0:T(8,128)(2,1)S(1)} fusion(f32[6,512,2048]{2,1,0:T(8,128)} %get-tuple-element.400, f32[6,512,2048]{2,1,0:T(8,128)} %fusion.150, f32[6,512]{1,0:T(8,128)S(1)} %get-tuple-element.401, f32[6,512]{1,0:T(8,128)S(1)} %dynamic-slice_bitcast_fusion.2, pred[512,2048]{1,0:T(8,128)(4,1)} %copy-done), kind=kLoop, calls=%fused_computation.24.clone.1 | loop fusion | flops 37748736 | bytes 63987712 | tf_op jit(solution)/shard_map/while/body/eval_jaxpr/convert_element_type | solution.py:206
  546.4 6.2 fusion.151
  557.5 11.9 %fusion.150 = f32[6,512,2048]{2,1,0:T(8,128)} fusion(bf16[2,2048,6,64]{1,3,2,0:T(8,128)(2,1)} %get-tuple-element.459, s32[]{:T(128)S(6)} %copy.91, bf16[2,512,6,64]{1,3,2,0:T(8,128)(2,1)S(1)} %get-tuple-element.462), kind=kOutput, calls=%fused_computation.36.clone.1 | convolution fusion | flops 805306368 | bytes 27132928 | tf_op jit(solution)/shard_map/while/body/eval_jaxpr/qhd,khd->hqk/dot_general | solution.py:64
  569.4 12.8 %fusion.152 = bf16[6,64,2048]{2,1,0:T(8,128)(2,1)} fusion(f32[6,512,2048]{2,1,0:T(8,128)} %fusion.150, f32[6,512]{1,0:T(8,128)S(1)} %dynamic-slice_bitcast_fusion.2, pred[512,2048]{1,0:T(8,128)(4,1)S(1)} %broadcast_compare_fusion.5, bf16[2,512,6,64]{1,3,2,0:T(8,128)(2,1)S(1)} %get-tuple-element.464, s32[]{:T(128)S(6)} %copy.91), kind=kOutput, calls=%fused_computation.28.clone.1 | convolution fusion | flops 830472192 | bytes 28196868 | tf_op jit(solution)/shard_map/while/body/eval_jaxpr/hqk,qhd->khd/dot_general | solution.py:215
  582.2 20.0 %multiply_reduce_fusion.7 = (f32[6,512]{1,0:T(8,128)S(1)}, f32[6,512,2048]{2,1,0:T(8,128)}) fusion(f32[6,512,2048]{2,1,0:T(8,128)} %fusion.150, f32[6,512]{1,0:T(8,128)S(1)} %dynamic-slice_bitcast_fusion.2, pred[512,2048]{1,0:T(8,128)(4,1)S(1)} %broadcast_compare_fusion.5, bf16[2,2048,6,64]{1,3,2,0:T(8,128)(2,1)} %get-tuple-element.465, ...), kind=kOutput, calls=%fused_computation.25.clone.1 | convolution fusion | flops 836760576 | bytes 53376000 | tf_op jit(solution)/shard_map/while/body/eval_jaxpr/qhd,khd->hqk/dot_general | solution.py:202
  602.3 17.7 %multiply_convert_fusion.5 = bf16[6,512,2048]{2,1,0:T(8,128)(2,1)S(1)} fusion(f32[6,512,2048]{2,1,0:T(8,128)} %get-tuple-element.400, f32[6,512,2048]{2,1,0:T(8,128)} %fusion.150, f32[6,512]{1,0:T(8,128)S(1)} %get-tuple-element.401, f32[6,512]{1,0:T(8,128)S(1)} %dynamic-slice_bitcast_fusion.2, pred[512,2048]{1,0:T(8,128)(4,1)} %copy-done), kind=kLoop, calls=%fused_computation.24.clone.1 | loop fusion | flops 37748736 | bytes 63987712 | tf_op jit(solution)/shard_map/while/body/eval_jaxpr/convert_element_type | solution.py:206
  624.4 6.3 fusion.151
  639.3 57.4 %reduce-scatter.10.cloned.1.call-done = bf16[2,512,384]{1,2,0:T(8,128)(2,1)} async-done(((bf16[2,2048,384]{1,2,0:T(8,128)(2,1)}), bf16[2,512,384]{1,2,0:T(8,128)(2,1)}) %reduce-scatter.10.cloned.1.call-update) | async-done | bytes 786448 | tf_op jit(solution)/shard_map/reduce_scatter | solution.py:227
  711.1 48.3 %reduce-scatter.12.cloned.1.call-done = bf16[2,512,384]{1,2,0:T(8,128)(2,1)} async-done(((bf16[2,2048,384]{1,2,0:T(8,128)(2,1)}), bf16[2,512,384]{1,2,0:T(8,128)(2,1)}) %reduce-scatter.12.cloned.1.call-update) | async-done | bytes 786448 | tf_op jit(solution)/shard_map/reduce_scatter | solution.py:230
  773.9 7.0 convolution_convert_fusion
  781.0 5.9 convolution_convert_fusion.2
  787.0 5.9 convolution_convert_fusion.1
  793.1 5.0 bitcast_convert_fusion
  798.2 4.9 reduce-scatter.22.cloned.1.call-done
  805.2 26.8 %reduce-scatter.14.cloned.1.call-done = bf16[192,384]{1,0:T(8,128)(2,1)} async-done(((bf16[768,384]{1,0:T(8,128)(2,1)}), bf16[192,384]{1,0:T(8,128)(2,1)}) %reduce-scatter.14.cloned.1.call-update) | async-done | bytes 147472 | tf_op jit(solution)/shard_map/reduce_scatter | solution.py:252
  832.0 40.3 %reduce-scatter.20.cloned.1.call-done = bf16[192,1536]{1,0:T(8,128)(2,1)} async-done(((bf16[768,1536]{1,0:T(8,128)(2,1)}), bf16[192,1536]{1,0:T(8,128)(2,1)}) %reduce-scatter.20.cloned.1.call-update) | async-done | bytes 589840 | tf_op jit(solution)/shard_map/reduce_scatter | solution.py:261
  872.3 40.3 %reduce-scatter.16.cloned.1.call-done = bf16[192,1536]{1,0:T(8,128)(2,1)} async-done(((bf16[768,1536]{1,0:T(8,128)(2,1)}), bf16[192,1536]{1,0:T(8,128)(2,1)}) %reduce-scatter.16.cloned.1.call-update) | async-done | bytes 589840 | tf_op jit(solution)/shard_map/reduce_scatter | solution.py:255
  912.6 40.3 %reduce-scatter.18.cloned.1.call-done = bf16[192,1536]{1,0:T(8,128)(2,1)} async-done(((bf16[768,1536]{1,0:T(8,128)(2,1)}), bf16[192,1536]{1,0:T(8,128)(2,1)}) %reduce-scatter.18.cloned.1.call-update) | async-done | bytes 589840 | tf_op jit(solution)/shard_map/reduce_scatter | solution.py:258
  955.6 15.0 %all-reduce.10 = (bf16[768]{0:T(1024)(128)(2,1)S(1)}, bf16[768]{0:T(1024)(128)(2,1)S(1)}, bf16[768]{0:T(1024)(128)(2,1)S(1)}, bf16[768]{0:T(1024)(128)(2,1)S(1)}, bf16[768]{0:T(1024)(128)(2,1)S(1)}) all-reduce(bf16[768]{0:T(1024)(128)(2,1)S(1)} %dynamic-update-slice.3, ...), channel_id=1, replica_groups=mesh['dp'=4,'ctx'=4,'tp'=2] {'dp'}, use_global_device_ids=true, to_apply=%add.3 | all-reduce | flops 3840 | bytes 15360
  970.9 11.7 %all-reduce.8 = (bf16[192]{0:T(256)(128)(2,1)S(1)}, bf16[192]{0:T(256)(128)(2,1)S(1)}, bf16[192]{0:T(256)(128)(2,1)S(1)}, bf16[192]{0:T(256)(128)(2,1)S(1)}) all-reduce(bf16[192]{0:T(256)(128)(2,1)S(1)} %dynamic-slice.5, bf16[192]{0:T(256)(128)(2,1)S(1)} %dynamic-slice.7, ...), channel_id=1, replica_groups=mesh['dp'=4,'ctx'=4,'tp'=2] {'ctx'}, use_global_device_ids=true, to_apply=%region_33.34 | all-reduce | flops 768 | bytes 3072 | tf_op jit(solution)/shard_map/psum | solution.py:283
  990.4 90.7 %all-reduce.26.cloned.1.call-done = (bf16[192,3,384]{0,2,1:T(8,128)(2,1)}, bf16[192,384]{1,0:T(8,128)(2,1)}, bf16[192,1536]{1,0:T(8,128)(2,1)}, bf16[192,1536]{1,0:T(8,128)(2,1)}, bf16[192,1536]{1,0:T(8,128)(2,1)}) async-done(((bf16[192,3,384]{0,2,1:T(8,128)(2,1)}, bf16[192,384]{1,0:T(8,128)(2,1)}, bf16[192,1536]{1,0:T(8,128)(2,1)}, bf16[192,1536]{1,0:T(8,128)(2,1)}, bf16[192,1536]{1,0:T(8,128)(2,1)}), ...) | async-done | bytes 2359312 | tf_op jit(solution)/shard_map/psum | solution.py:278
  (282 shorter events, 130.0 us)
Async XLA Ops:
  7.2 40.5 %copy-start.5 = (bf16[2,512,768]{2,1,0:T(8,128)(2,1)S(1)}, bf16[2,512,768]{2,1,0:T(8,128)(2,1)}, u32[]{:S(2)}) copy-start(bf16[2,512,768]{2,1,0:T(8,128)(2,1)} %param.16) | copy-start | bytes 4718596
  7.2 37.9 %all-gather.7.cloned.1.call-start = ((), (), s32[]{:S(2)}) async-start(), calls=%async_computation.7 | async-start | bytes 2211840 | tf_op jit(solution)/shard_map/all_gather | solution.py:87
  7.9 108.7 %all-gather.9.cloned.1.call-start = ((), (), s32[]{:S(2)}) async-start(), calls=%async_computation.8 | async-start | bytes 3932160 | tf_op jit(solution)/shard_map/all_gather | solution.py:123
  52.9 128.0 %all-gather.11.cloned.1.call-start = ((), (), s32[]{:S(2)}) async-start(), calls=%async_computation.9 | async-start | bytes 3932160 | tf_op jit(solution)/shard_map/all_gather | solution.py:122
  53.3 29.7 %copy-start.22 = (f32[512,64]{0,1:T(8,128)}, f32[512,64]{0,1:T(8,128)S(1)}, u32[]{:S(2)}) copy-start(f32[512,64]{0,1:T(8,128)S(1)} %get-tuple-element.268) | copy-start | bytes 393220
  53.3 29.7 %copy-start.27 = (f32[512,64]{0,1:T(8,128)}, f32[512,64]{0,1:T(8,128)S(1)}, u32[]{:S(2)}) copy-start(f32[512,64]{0,1:T(8,128)S(1)} %get-tuple-element.269) | copy-start | bytes 393220
  56.2 15.2 %copy-start.35 = (bf16[192,384]{1,0:T(8,128)(2,1)S(1)}, bf16[192,384]{1,0:T(8,128)(2,1)}, u32[]{:S(2)}) copy-start(bf16[192,384]{1,0:T(8,128)(2,1)} %param.20) | copy-start | bytes 442372
  57.8 219.7 %all-reduce.18.cloned.1.call-start = ((), (), s32[]{:S(2)}) async-start(), calls=%async_computation.10 | async-start | bytes 3145728 | tf_op jit(solution)/shard_map/psum | solution.py:142
  193.8 12.1 %copy-start.15 = (bf16[2,2048,6,64]{1,3,2,0:T(8,128)(2,1)S(1)}, bf16[2,2048,6,64]{1,3,2,0:T(8,128)(2,1)}, u32[]{:S(2)}) copy-start(bf16[2,2048,6,64]{1,3,2,0:T(8,128)(2,1)} %get-tuple-element.425) | copy-start | bytes 9437188 | tf_op jit(solution)/shard_map/while
  230.4 12.1 %copy-start.15 = (bf16[2,2048,6,64]{1,3,2,0:T(8,128)(2,1)S(1)}, bf16[2,2048,6,64]{1,3,2,0:T(8,128)(2,1)}, u32[]{:S(2)}) copy-start(bf16[2,2048,6,64]{1,3,2,0:T(8,128)(2,1)} %get-tuple-element.425) | copy-start | bytes 9437188 | tf_op jit(solution)/shard_map/while
  256.1 21.4 %copy-start.6 = (bf16[2,512,768]{2,1,0:T(8,128)(2,1)S(1)}, bf16[2,512,768]{2,1,0:T(8,128)(2,1)}, u32[]{:S(2)}) copy-start(bf16[2,512,768]{2,1,0:T(8,128)(2,1)} %param.16) | copy-start | bytes 4718596
  258.3 59.4 %all-gather.13.cloned.1.call-start = ((), (), s32[]{:S(2)}) async-start(), calls=%async_computation.11 | async-start | bytes 2949120 | tf_op jit(solution)/shard_map/all_gather | solution.py:89
  258.9 97.9 %all-gather.15.cloned.1.call-start = ((), (), s32[]{:S(2)}) async-start(), calls=%async_computation.12 | async-start | bytes 2949120 | tf_op jit(solution)/shard_map/all_gather | solution.py:90
  259.5 136.5 %all-gather.17.cloned.1.call-start = ((), (), s32[]{:S(2)}) async-start(), calls=%async_computation.13 | async-start | bytes 2949120 | tf_op jit(solution)/shard_map/all_gather | solution.py:91
  260.3 162.7 %all-reduce.20.cloned.1.call-start = ((), (), s32[]{:S(2)}) async-start(), calls=%async_computation.14 | async-start | bytes 3145728 | tf_op jit(solution)/shard_map/psum | solution.py:154
  402.4 65.5 %all-reduce.22.cloned.1.call-start = ((), (), s32[]{:S(2)}) async-start(), calls=%async_computation.15 | async-start | bytes 3145728 | tf_op jit(solution)/shard_map/psum | solution.py:191
  403.0 27.4 %copy-start.36 = (f32[768]{0:T(1024)}, f32[768]{0:T(1024)S(1)}, u32[]{:S(2)}) copy-start(f32[768]{0:T(1024)S(1)} %convert_element_type.216) | copy-start | bytes 9220
  431.6 7.4 copy-start.12
  432.1 6.9 copy-start.46
  446.2 250.5 %reduce-scatter.10.cloned.1.call-start = ((), (), s32[]{:S(2)}) async-start(), calls=%async_computation.16 | async-start | bytes 3932160 | tf_op jit(solution)/shard_map/reduce_scatter | solution.py:227
  478.7 12.7 %copy-start.3 = (bf16[2,512,6,64]{1,3,2,0:T(8,128)(2,1)}, bf16[2,512,6,64]{1,3,2,0:T(8,128)(2,1)S(1)}, u32[]{:S(2)}) copy-start(bf16[2,512,6,64]{1,3,2,0:T(8,128)(2,1)S(1)} %get-tuple-element.462) | copy-start | bytes 2359300 | tf_op jit(solution)/shard_map/while
  478.7 25.5 %copy-start.16 = (bf16[2,512,6,64]{1,3,2,0:T(8,128)(2,1)}, bf16[2,512,6,64]{1,3,2,0:T(8,128)(2,1)S(1)}, u32[]{:S(2)}) copy-start(bf16[2,512,6,64]{1,3,2,0:T(8,128)(2,1)S(1)} %get-tuple-element.464) | copy-start | bytes 2359300 | tf_op jit(solution)/shard_map/while
  479.5 24.8 %copy-start = (pred[512,2048]{1,0:T(8,128)(4,1)}, pred[512,2048]{1,0:T(8,128)(4,1)S(1)}, u32[]{:S(2)}) copy-start(pred[512,2048]{1,0:T(8,128)(4,1)S(1)} %broadcast_compare_fusion.5) | copy-start | bytes 3145732 | tf_op jit(solution)/shard_map/while
  556.7 12.7 %copy-start.3 = (bf16[2,512,6,64]{1,3,2,0:T(8,128)(2,1)}, bf16[2,512,6,64]{1,3,2,0:T(8,128)(2,1)S(1)}, u32[]{:S(2)}) copy-start(bf16[2,512,6,64]{1,3,2,0:T(8,128)(2,1)S(1)} %get-tuple-element.462) | copy-start | bytes 2359300 | tf_op jit(solution)/shard_map/while
  556.7 25.5 %copy-start.16 = (bf16[2,512,6,64]{1,3,2,0:T(8,128)(2,1)}, bf16[2,512,6,64]{1,3,2,0:T(8,128)(2,1)S(1)}, u32[]{:S(2)}) copy-start(bf16[2,512,6,64]{1,3,2,0:T(8,128)(2,1)S(1)} %get-tuple-element.464) | copy-start | bytes 2359300 | tf_op jit(solution)/shard_map/while
  557.5 24.8 %copy-start = (pred[512,2048]{1,0:T(8,128)(4,1)}, pred[512,2048]{1,0:T(8,128)(4,1)S(1)}, u32[]{:S(2)}) copy-start(pred[512,2048]{1,0:T(8,128)(4,1)S(1)} %broadcast_compare_fusion.5) | copy-start | bytes 3145732 | tf_op jit(solution)/shard_map/while
  635.0 124.4 %reduce-scatter.12.cloned.1.call-start = ((), (), s32[]{:S(2)}) async-start(), calls=%async_computation.17 | async-start | bytes 3932160 | tf_op jit(solution)/shard_map/reduce_scatter | solution.py:230
  635.7 167.4 %reduce-scatter.22.cloned.1.call-start = ((), (), s32[]{:S(2)}) async-start(), calls=%async_computation.23 | async-start | bytes 2211840
  637.6 60.5 %copy-start.21 = (f32[2,512,6,64]{1,3,2,0:T(8,128)S(1)}, f32[2,512,6,64]{1,3,2,0:T(8,128)}, u32[]{:S(2)}) copy-start(f32[2,512,6,64]{1,3,2,0:T(8,128)} %get-tuple-element.115) | copy-start | bytes 4718596
  637.6 60.5 %copy-start.28 = (f32[512,64]{0,1:T(8,128)S(1)}, f32[512,64]{0,1:T(8,128)}, u32[]{:S(2)}) copy-start(f32[512,64]{0,1:T(8,128)} %copy-done.27) | copy-start | bytes 393220
  708.0 53.8 %copy-start.7 = (bf16[2,512,768]{2,1,0:T(8,128)(2,1)S(1)}, bf16[2,512,768]{2,1,0:T(8,128)(2,1)}, u32[]{:S(2)}) copy-start(bf16[2,512,768]{2,1,0:T(8,128)(2,1)} %param.16) | copy-start | bytes 4718596
  770.6 61.5 %reduce-scatter.14.cloned.1.call-start = ((), (), s32[]{:S(2)}) async-start(), calls=%async_computation.19 | async-start | bytes 737280 | tf_op jit(solution)/shard_map/reduce_scatter | solution.py:252
  773.9 7.2 copy-start.30
  773.9 98.4 %reduce-scatter.20.cloned.1.call-start = ((), (), s32[]{:S(2)}) async-start(), calls=%async_computation.22 | async-start | bytes 2949120 | tf_op jit(solution)/shard_map/reduce_scatter | solution.py:261
  781.0 131.6 %reduce-scatter.16.cloned.1.call-start = ((), (), s32[]{:S(2)}) async-start(), calls=%async_computation.20 | async-start | bytes 2949120 | tf_op jit(solution)/shard_map/reduce_scatter | solution.py:255
  787.0 166.0 %reduce-scatter.18.cloned.1.call-start = ((), (), s32[]{:S(2)}) async-start(), calls=%async_computation.21 | async-start | bytes 2949120 | tf_op jit(solution)/shard_map/reduce_scatter | solution.py:258
  793.0 193.6 %all-reduce.24.cloned.1.call-start = ((), (), s32[]{:S(2)}) async-start(), calls=%async_computation.18 | async-start | bytes 3145728 | tf_op jit(solution)/shard_map/psum | solution.py:244
  798.1 157.3 %copy-start.52 = (bf16[192]{0:T(256)(128)(2,1)S(1)}, bf16[192]{0:T(256)(128)(2,1)}, u32[]{:S(2)}) copy-start(bf16[192]{0:T(256)(128)(2,1)} %param.27) | copy-start | bytes 1156
  798.1 157.5 %copy-start.42 = (bf16[768]{0:T(1024)(128)(2,1)S(1)}, bf16[768]{0:T(1024)(128)(2,1)}, u32[]{:S(2)}) copy-start(bf16[768]{0:T(1024)(128)(2,1)} %get-tuple-element.186) | copy-start | bytes 4612
  798.1 157.5 %copy-start.43 = (bf16[768]{0:T(1024)(128)(2,1)S(1)}, bf16[768]{0:T(1024)(128)(2,1)}, u32[]{:S(2)}) copy-start(bf16[768]{0:T(1024)(128)(2,1)} %get-tuple-element.184) | copy-start | bytes 4612
  798.1 157.5 %copy-start.44 = (bf16[768]{0:T(1024)(128)(2,1)S(1)}, bf16[768]{0:T(1024)(128)(2,1)}, u32[]{:S(2)}) copy-start(bf16[768]{0:T(1024)(128)(2,1)} %get-tuple-element.189) | copy-start | bytes 4612
  798.1 186.8 %copy-start.2 = (f32[1024,768]{1,0:T(8,128)S(1)}, f32[1024,768]{1,0:T(8,128)}, u32[]{:S(2)}) copy-start(f32[1024,768]{1,0:T(8,128)} %copy-done.1) | copy-start | bytes 9437188
  798.1 186.8 %copy-start.37 = (f32[768]{0:T(1024)S(1)}, f32[768]{0:T(1024)}, u32[]{:S(2)}) copy-start(f32[768]{0:T(1024)} %copy-done.36) | copy-start | bytes 9220
  798.1 186.8 %copy-start.39 = (f32[1024]{0:T(1024)S(1)}, f32[1024]{0:T(1024)}, u32[]{:S(2)}) copy-start(f32[1024]{0:T(1024)} %copy-done.38) | copy-start | bytes 12292
  798.1 186.8 %copy-start.41 = (f32[1024]{0:T(1024)S(1)}, f32[1024]{0:T(1024)}, u32[]{:S(2)}) copy-start(f32[1024]{0:T(1024)} %copy-done.40) | copy-start | bytes 12292
  798.1 283.0 %all-reduce.26.cloned.1.call-start = ((), (), s32[]{:S(2)}) async-start(), calls=%async_computation.24 | async-start | bytes 5013504 | tf_op jit(solution)/shard_map/psum | solution.py:278
  1081.1 6.2 copy-start.33
  1081.1 7.3 copy-start.32
  (33 other events, 113.0 us)
Sparse Core Ops, SparseCore 0:
  9.8 35.1 all-gather.6
  53.0 63.5 all-gather.8
  118.8 62.0 all-gather.10
  258.5 18.9 all-reduce.17
  279.2 38.5 all-gather.12
  319.4 37.3 all-gather.14
  358.6 37.3 all-gather.16
  402.6 20.3 all-reduce.19
  446.3 21.5 all-reduce.21
  635.1 61.5 reduce-scatter.9
  699.1 60.3 reduce-scatter.11
  770.7 32.3 reduce-scatter.21
  806.5 25.4 reduce-scatter.13
  834.9 37.3 reduce-scatter.19
  875.2 37.3 reduce-scatter.15
  915.5 37.3 reduce-scatter.17
  955.7 20.3 all-reduce.23
  979.3 101.7 all-reduce.25
where the time goes:
time: 1100 us
  waiting for transfers between devices  626 us (57%)
  matrix products  233 us (21%)
  other arithmetic  108 us (10%)
  blocking collectives  62 us (6%)
  local copies, waits for them, and re-layouts  49.2 us (4%)
  between operations  16.9 us (2%)
    psum x1, waiting for transfers between devices, body(): lax.psum(group_part[0].astype(jnp.bfloat16), 'ctx').astype(jnp.float32)  90.7 us
    all_gather x1, waiting for transfers between devices, body(): lax.all_gather(keys_rot, 'ctx', axis=1, tiled=True)  64.3 us
    reduce_scatter x1, waiting for transfers between devices, body(): lax.psum_scatter(dkeys_all.astype(jnp.bfloat16), 'ctx', scatter_dimension...  57.4 us
    reduce_scatter x1, waiting for transfers between devices, body(): lax.psum_scatter(dvalues_all.astype(jnp.bfloat16), 'ctx', scatter_dimensi...  48.3 us
    dot_general x4, matrix products, masked_scores(): jnp.einsum('qhd,khd->hqk', queries, keys_rot, preferred_element_type=jnp....  48.2 us
    reduce_scatter x1, waiting for transfers between devices, body(): lax.psum_scatter(grad_terms[3].astype(jnp.bfloat16), 'dp', scatter_dimens...  40.3 us
    reduce_scatter x1, waiting for transfers between devices, body(): lax.psum_scatter(grad_terms[2].astype(jnp.bfloat16), 'dp', scatter_dimens...  40.3 us
    reduce_scatter x1, waiting for transfers between devices, body(): lax.psum_scatter(grad_terms[4].astype(jnp.bfloat16), 'dp', scatter_dimens...  40.3 us
  transfers between devices with their start and end apart: 18, of which 17 were waited for; matrix products, arithmetic and copies ran while one was open for 8% of the time, Pallas kernels for 0%

commit v1 on v0

--- a/solution.py
+++ b/solution.py
@@ -6,6 +6,18 @@
 HD = 64
 epsilon = 1e-12
 rotary_base = 1000.0
+
+
+def collect(x, axis, dim):
+    ways, here = (lax.axis_size(axis), lax.axis_index(axis))
+    grown, reach = (x, 1)
+    while reach < ways:
+        theirs = lax.ppermute(grown, axis, [(d, d ^ reach) for d in range(ways)])
+        mine_first = jnp.concatenate([grown, theirs], axis=dim)
+        theirs_first = jnp.concatenate([theirs, grown], axis=dim)
+        grown = jnp.where(here & reach == 0, mine_first, theirs_first)
+        reach = 2 * reach
+    return grown
 
 
 def rotary_tables(offset, length, head_size):
@@ -119,7 +131,7 @@
     )
     valued = pieces[:, :, 2].astype(jnp.bfloat16).reshape(seq_count, row_count, local_width)
     all_keys, all_values = (
-        lax.all_gather(keys_rot, "ctx", axis=1, tiled=True),
+        collect(keys_rot, "ctx", 1),
         lax.all_gather(valued, "ctx", axis=1, tiled=True),
     )
     all_docs = lax.all_gather(segments, "ctx", axis=1, tiled=True)

time: 1100 us -> 1150 us (1.045)
  blocking collectives: 62 us -> 123 us
  waiting for transfers between devices: 626 us -> 587 us
  local copies, waits for them, and re-layouts: 49.2 us -> 62.7 us
    all_gather x1 -> x0, waiting for transfers between devices: 64.3 us -> none  [body(): lax.all_gather(keys_rot, 'ctx', axis=1, tiled=True)]
    all_gather x1, blocking collectives: 13.6 us -> 76.1 us  [body(): all_docs = lax.all_gather(segments, 'ctx', axis=1, tiled=True)]
    ppermute x0 -> x2, waiting for transfers between devices: none -> 58.8 us  [collect(): theirs = lax.ppermute(grown, axis, [(d, d ^ reach) for d in range(ways)])]
    all_gather x1, waiting for transfers between devices: 31.7 us -> 0.02 us  [body(): lax.all_gather(valued, 'ctx', axis=1, tiled=True)]
  transfers between devices with their start and end apart: 18 -> 19, of which waited for: 17 -> 16; matrix products, arithmetic and copies ran while one was open for 8% -> 8% of each run, Pallas kernels for 0% -> 0%
where the time goes in v1:
time: 1150 us; the launch traced here: 1140 us
  waiting for transfers between devices  587 us (51%)
  matrix products  236 us (21%)
  blocking collectives  123 us (11%)
  other arithmetic  113 us (10%)
  local copies, waits for them, and re-layouts  62.7 us (5%)
  between operations  16.3 us (1%)
    psum x1, waiting for transfers between devices, body(): lax.psum(group_part[0].astype(jnp.bfloat16), 'ctx').astype(jnp.float32)  90.7 us
    all_gather x1, blocking collectives, body(): all_docs = lax.all_gather(segments, 'ctx', axis=1, tiled=True)  76.1 us
    ppermute x2, waiting for transfers between devices, collect(): theirs = lax.ppermute(grown, axis, [(d, d ^ reach) for d in range(ways)])  58.8 us
    reduce_scatter x1, waiting for transfers between devices, body(): lax.psum_scatter(dkeys_all.astype(jnp.bfloat16), 'ctx', scatter_dimension...  57.4 us
    dot_general x4, matrix products, masked_scores(): jnp.einsum('qhd,khd->hqk', queries, keys_rot, preferred_element_type=jnp....  50.7 us
    reduce_scatter x1, waiting for transfers between devices, body(): lax.psum_scatter(dvalues_all.astype(jnp.bfloat16), 'ctx', scatter_dimensi...  48.1 us
    reduce_scatter x1, waiting for transfers between devices, body(): lax.psum_scatter(grad_terms[4].astype(jnp.bfloat16), 'dp', scatter_dimens...  40.5 us
    reduce_scatter x1, waiting for transfers between devices, body(): lax.psum_scatter(grad_terms[3].astype(jnp.bfloat16), 'dp', scatter_dimens...  40.3 us
  transfers between devices with their start and end apart: 19, of which 16 were waited for; matrix products, arithmetic and copies ran while one was open for 8% of the time, Pallas kernels for 0%

profile of v1, /device:TPU:0, one launch (start us, length us, event | category | flops | bytes accessed | tf_op | source)
XLA Modules:
  0.0 1144.1 jit_solution(3720865042750576043)
XLA Ops:
  8.0 37.1 %all-gather.6.cloned.1.call-done = bf16[768,3,384]{2,0,1:T(8,128)(2,1)} async-done(((bf16[192,3,384]{2,0,1:T(8,128)(2,1)}), bf16[768,3,384]{2,0,1:T(8,128)(2,1)}) %all-gather.6.cloned.1.call-update) | async-done | bytes 1769488 | tf_op jit(solution)/shard_map/all_gather | solution.py:99
  60.7 58.8 %collective-permute-done = bf16[2,512,384]{1,2,0:T(8,128)(2,1)S(1)} collective-permute-done((bf16[2,512,384]{1,2,0:T(8,128)(2,1)S(1)}, bf16[2,512,384]{1,2,0:T(8,128)(2,1)S(1)}, u32[]{:S(2)}, u32[]{:S(2)}) %collective-permute-start) | collective-permute-done | bytes 786464 | tf_op jit(solution)/shard_map/ppermute | solution.py:15
  123.5 76.1 %all_gather.42 = s32[2,2048]{1,0:T(2,128)S(1)} all-gather(s32[2,512]{1,0:T(2,128)S(1)} %copy-done.37), channel_id=1, replica_groups=mesh['dp'=4,'ctx'=4,'tp'=2] {'ctx'}, dimensions={1}, use_global_device_ids=true | all-gather | bytes 20480 | tf_op jit(solution)/shard_map/all_gather | solution.py:137
  199.6 11.3 all_gather.43
  215.7 73.6 %while.26 = (s32[]{:T(128)}, bf16[2,512,6,64]{1,3,2,0:T(8,128)(2,1)}, f32[2,6,512]{2,1,0:T(8,128)S(1)}, bf16[2,2048,6,64]{1,3,2,0:T(8,128)(2,1)}, s32[2,512]{1,0...) while((s32[]{:T(128)}, ...), condition=%wide.region_3.4_spmd, body=%wide.region_0.3_spmd.sunk | while | flops 1687352320 | bytes 96358544 | solution.py:152
  216.4 11.7 %fusion.139 = (f32[6,512]{1,0:T(8,128)S(1)}, f32[6,512,2048]{2,1,0:T(8,128)}) fusion(pred[512,2048]{1,0:T(8,128)(4,1)S(1)} %broadcast_compare_fusion.4, bf16[2,2048,6,64]{1,3,2,0:T(8,128)(2,1)S(1)} %get-tuple-element.432, s32[]{:T(128)S(6)} %copy.81, bf16[2,512,6,64]{1,3,2,0:T(8,128)(2,1)} %get-tuple-element.431), kind=kOutput, calls=%fused_computation.3.clone.1 | convolution fusion | flops 824177664 | bytes 28193792 | tf_op jit(solution)/shard_map/while/body/eval_jaxpr/qhd,khd->hqk/dot_general | solution.py:76
  228.0 12.1 %fusion.140 = f32[6,512]{1,0:T(8,128)S(1)} fusion(f32[6,512,2048]{2,1,0:T(8,128)} %get-tuple-element.390, f32[6,512]{1,0:T(8,128)S(1)} %get-tuple-element.391, pred[512,2048]{1,0:T(8,128)(4,1)S(1)} %broadcast_compare_fusion.4), kind=kLoop, calls=%fused_computation.4.clone.1 | loop fusion | flops 25162752 | bytes 26238976 | tf_op jit(solution)/shard_map/while/body/eval_jaxpr/reduce_sum | solution.py:147
  240.2 12.3 %fusion.141 = bf16[2,512,6,64]{1,3,2,0:T(8,128)(2,1)} fusion(bf16[2,512,6,64]{1,3,2,0:T(8,128)(2,1)} %get-tuple-element.417, s32[]{:T(128)S(6)} %copy.81, f32[6,512,2048]{2,1,0:T(8,128)} %get-tuple-element.390, f32[6,512]{1,0:T(8,128)S(1)} %fusion.140, f32[6,512]{1,0:T(8,128)S(1)} %get-tuple-element.391, ...), kind=kOutput, calls=%fused_computation.14.clone.1 | convolution fusion | flops 836960256 | bytes 28214272 | tf_op jit(solution)/shard_map/while/body/eval_jaxpr/hqk,khd->qhd/dot_general | solution.py:149
  253.2 11.7 %fusion.139 = (f32[6,512]{1,0:T(8,128)S(1)}, f32[6,512,2048]{2,1,0:T(8,128)}) fusion(pred[512,2048]{1,0:T(8,128)(4,1)S(1)} %broadcast_compare_fusion.4, bf16[2,2048,6,64]{1,3,2,0:T(8,128)(2,1)S(1)} %get-tuple-element.432, s32[]{:T(128)S(6)} %copy.81, bf16[2,512,6,64]{1,3,2,0:T(8,128)(2,1)} %get-tuple-element.431), kind=kOutput, calls=%fused_computation.3.clone.1 | convolution fusion | flops 824177664 | bytes 28193792 | tf_op jit(solution)/shard_map/while/body/eval_jaxpr/qhd,khd->hqk/dot_general | solution.py:76
  264.9 12.1 %fusion.140 = f32[6,512]{1,0:T(8,128)S(1)} fusion(f32[6,512,2048]{2,1,0:T(8,128)} %get-tuple-element.390, f32[6,512]{1,0:T(8,128)S(1)} %get-tuple-element.391, pred[512,2048]{1,0:T(8,128)(4,1)S(1)} %broadcast_compare_fusion.4), kind=kLoop, calls=%fused_computation.4.clone.1 | loop fusion | flops 25162752 | bytes 26238976 | tf_op jit(solution)/shard_map/while/body/eval_jaxpr/reduce_sum | solution.py:147
  277.0 12.3 %fusion.141 = bf16[2,512,6,64]{1,3,2,0:T(8,128)(2,1)} fusion(bf16[2,512,6,64]{1,3,2,0:T(8,128)(2,1)} %get-tuple-element.417, s32[]{:T(128)S(6)} %copy.81, f32[6,512,2048]{2,1,0:T(8,128)} %get-tuple-element.390, f32[6,512]{1,0:T(8,128)S(1)} %fusion.140, f32[6,512]{1,0:T(8,128)S(1)} %get-tuple-element.391, ...), kind=kOutput, calls=%fused_computation.14.clone.1 | convolution fusion | flops 836960256 | bytes 28214272 | tf_op jit(solution)/shard_map/while/body/eval_jaxpr/hqk,khd->qhd/dot_general | solution.py:149
  298.3 9.3 all-reduce.11
  317.9 34.6 %all-gather.10.cloned.1.call-done = bf16[768,1536]{1,0:T(8,128)(2,1)} async-done(((bf16[192,1536]{1,0:T(8,128)(2,1)}), bf16[768,1536]{1,0:T(8,128)(2,1)}) %all-gather.10.cloned.1.call-update) | async-done | bytes 2359312 | tf_op jit(solution)/shard_map/all_gather | solution.py:101
  352.6 7.4 fusion.96
  360.0 31.6 %all-gather.12.cloned.1.call-done = bf16[768,1536]{1,0:T(8,128)(2,1)} async-done(((bf16[192,1536]{1,0:T(8,128)(2,1)}), bf16[768,1536]{1,0:T(8,128)(2,1)}) %all-gather.12.cloned.1.call-update) | async-done | bytes 2359312 | tf_op jit(solution)/shard_map/all_gather | solution.py:102
  391.6 10.6 multiply_convert_fusion.3
  402.2 28.5 %all-gather.14.cloned.1.call-done = bf16[768,1536]{1,0:T(8,128)(2,1)} async-done(((bf16[192,1536]{1,0:T(8,128)(2,1)}), bf16[768,1536]{1,0:T(8,128)(2,1)}) %all-gather.14.cloned.1.call-update) | async-done | bytes 2359312 | tf_op jit(solution)/shard_map/all_gather | solution.py:103
  430.7 6.4 convolution_convert_fusion.5
  439.4 18.2 %all-reduce.20.cloned.1.call-done = bf16[1024,768]{1,0:T(8,128)(2,1)} async-done(((bf16[1024,768]{1,0:T(8,128)(2,1)}), bf16[1024,768]{1,0:T(8,128)(2,1)}) %all-reduce.20.cloned.1.call-update) | async-done | bytes 1572880 | tf_op jit(solution)/shard_map/psum | solution.py:166
  467.3 6.8 multiply_convert_fusion.1
  481.4 21.6 %all-reduce.22.cloned.1.call-done = bf16[1024,768]{1,0:T(8,128)(2,1)} async-done(((bf16[1024,768]{1,0:T(8,128)(2,1)}), bf16[1024,768]{1,0:T(8,128)(2,1)}) %all-reduce.22.cloned.1.call-update) | async-done | bytes 1572880 | tf_op jit(solution)/shard_map/psum | solution.py:203
  503.1 5.0 multiply_reduce_fusion.1
  521.5 161.5 %while.27 = (s32[]{:T(128)}, f32[2,512,6,64]{1,3,2,0:T(8,128)}, bf16[2,2048,384]{1,2,0:T(8,128)(2,1)}, bf16[2,2048,384]{1,2,0:T(8,128)(2,1)}, bf16[2,2048,6,64]{...) while((s32[]{:T(128)}, f32[2,512,6,64]{1,3,2,0:T(8,128)}, ...), condition=%wide.region_17.18_spmd, body=%wide.region_15.17_spmd.sunk | while | flops 4123718656 | bytes 245232944 | solution.py:235
  524.0 13.7 %fusion.150 = f32[6,512,2048]{2,1,0:T(8,128)} fusion(bf16[2,2048,6,64]{1,3,2,0:T(8,128)(2,1)} %copy-done.1, s32[]{:T(128)S(6)} %copy.95, bf16[2,512,6,64]{1,3,2,0:T(8,128)(2,1)} %get-tuple-element.465), kind=kOutput, calls=%fused_computation.36.clone.1 | convolution fusion | flops 805306368 | bytes 27132928 | tf_op jit(solution)/shard_map/while/body/eval_jaxpr/qhd,khd->hqk/dot_general | solution.py:76
  537.7 12.8 %fusion.152 = bf16[6,64,2048]{2,1,0:T(8,128)(2,1)} fusion(f32[6,512,2048]{2,1,0:T(8,128)} %fusion.150, f32[6,512]{1,0:T(8,128)S(1)} %dynamic-slice_bitcast_fusion.2, pred[512,2048]{1,0:T(8,128)(4,1)S(1)} %broadcast_compare_fusion.5, bf16[2,512,6,64]{1,3,2,0:T(8,128)(2,1)S(1)} %copy-done.19, s32[]{:T(128)S(6)} %copy.95), kind=kOutput, calls=%fused_computation.28.clone.1 | convolution fusion | flops 830472192 | bytes 28196868 | tf_op jit(solution)/shard_map/while/body/eval_jaxpr/hqk,qhd->khd/dot_general | solution.py:227
  550.5 20.0 %multiply_reduce_fusion.7 = (f32[6,512]{1,0:T(8,128)S(1)}, f32[6,512,2048]{2,1,0:T(8,128)}) fusion(f32[6,512,2048]{2,1,0:T(8,128)} %fusion.150, f32[6,512]{1,0:T(8,128)S(1)} %dynamic-slice_bitcast_fusion.2, pred[512,2048]{1,0:T(8,128)(4,1)S(1)} %broadcast_compare_fusion.5, bf16[2,2048,6,64]{1,3,2,0:T(8,128)(2,1)} %get-tuple-element.468, ...), kind=kOutput, calls=%fused_computation.25.clone.1 | convolution fusion | flops 836760576 | bytes 53376000 | tf_op jit(solution)/shard_map/while/body/eval_jaxpr/qhd,khd->hqk/dot_general | solution.py:214
  570.5 17.8 %multiply_convert_fusion.5 = bf16[6,512,2048]{2,1,0:T(8,128)(2,1)S(1)} fusion(f32[6,512,2048]{2,1,0:T(8,128)} %get-tuple-element.403, f32[6,512,2048]{2,1,0:T(8,128)} %fusion.150, f32[6,512]{1,0:T(8,128)S(1)} %get-tuple-element.404, f32[6,512]{1,0:T(8,128)S(1)} %dynamic-slice_bitcast_fusion.2, pred[512,2048]{1,0:T(8,128)(4,1)} %copy-done), kind=kLoop, calls=%fused_computation.24.clone.1 | loop fusion | flops 37748736 | bytes 63987712 | tf_op jit(solution)/shard_map/while/body/eval_jaxpr/convert_element_type | solution.py:218
  591.8 6.2 fusion.151
  604.5 13.7 %fusion.150 = f32[6,512,2048]{2,1,0:T(8,128)} fusion(bf16[2,2048,6,64]{1,3,2,0:T(8,128)(2,1)} %copy-done.1, s32[]{:T(128)S(6)} %copy.95, bf16[2,512,6,64]{1,3,2,0:T(8,128)(2,1)} %get-tuple-element.465), kind=kOutput, calls=%fused_computation.36.clone.1 | convolution fusion | flops 805306368 | bytes 27132928 | tf_op jit(solution)/shard_map/while/body/eval_jaxpr/qhd,khd->hqk/dot_general | solution.py:76
  618.2 12.8 %fusion.152 = bf16[6,64,2048]{2,1,0:T(8,128)(2,1)} fusion(f32[6,512,2048]{2,1,0:T(8,128)} %fusion.150, f32[6,512]{1,0:T(8,128)S(1)} %dynamic-slice_bitcast_fusion.2, pred[512,2048]{1,0:T(8,128)(4,1)S(1)} %broadcast_compare_fusion.5, bf16[2,512,6,64]{1,3,2,0:T(8,128)(2,1)S(1)} %copy-done.19, s32[]{:T(128)S(6)} %copy.95), kind=kOutput, calls=%fused_computation.28.clone.1 | convolution fusion | flops 830472192 | bytes 28196868 | tf_op jit(solution)/shard_map/while/body/eval_jaxpr/hqk,qhd->khd/dot_general | solution.py:227
  631.0 20.0 %multiply_reduce_fusion.7 = (f32[6,512]{1,0:T(8,128)S(1)}, f32[6,512,2048]{2,1,0:T(8,128)}) fusion(f32[6,512,2048]{2,1,0:T(8,128)} %fusion.150, f32[6,512]{1,0:T(8,128)S(1)} %dynamic-slice_bitcast_fusion.2, pred[512,2048]{1,0:T(8,128)(4,1)S(1)} %broadcast_compare_fusion.5, bf16[2,2048,6,64]{1,3,2,0:T(8,128)(2,1)} %get-tuple-element.468, ...), kind=kOutput, calls=%fused_computation.25.clone.1 | convolution fusion | flops 836760576 | bytes 53376000 | tf_op jit(solution)/shard_map/while/body/eval_jaxpr/qhd,khd->hqk/dot_general | solution.py:214
  651.0 17.8 %multiply_convert_fusion.5 = bf16[6,512,2048]{2,1,0:T(8,128)(2,1)S(1)} fusion(f32[6,512,2048]{2,1,0:T(8,128)} %get-tuple-element.403, f32[6,512,2048]{2,1,0:T(8,128)} %fusion.150, f32[6,512]{1,0:T(8,128)S(1)} %get-tuple-element.404, f32[6,512]{1,0:T(8,128)S(1)} %dynamic-slice_bitcast_fusion.2, pred[512,2048]{1,0:T(8,128)(4,1)} %copy-done), kind=kLoop, calls=%fused_computation.24.clone.1 | loop fusion | flops 37748736 | bytes 63987712 | tf_op jit(solution)/shard_map/while/body/eval_jaxpr/convert_element_type | solution.py:218
  672.2 6.3 fusion.151
  687.3 57.4 %reduce-scatter.10.cloned.1.call-done = bf16[2,512,384]{1,2,0:T(8,128)(2,1)} async-done(((bf16[2,2048,384]{1,2,0:T(8,128)(2,1)}), bf16[2,512,384]{1,2,0:T(8,128)(2,1)}) %reduce-scatter.10.cloned.1.call-update) | async-done | bytes 786448 | tf_op jit(solution)/shard_map/reduce_scatter | solution.py:239
  759.2 48.1 %reduce-scatter.12.cloned.1.call-done = bf16[2,512,384]{1,2,0:T(8,128)(2,1)} async-done(((bf16[2,2048,384]{1,2,0:T(8,128)(2,1)}), bf16[2,512,384]{1,2,0:T(8,128)(2,1)}) %reduce-scatter.12.cloned.1.call-update) | async-done | bytes 786448 | tf_op jit(solution)/shard_map/reduce_scatter | solution.py:242
  809.7 4.7 convolution_convert_fusion.3
  821.7 7.0 convolution_convert_fusion
  828.8 5.9 convolution_convert_fusion.2
  834.8 5.9 convolution_convert_fusion.1
  840.8 5.0 bitcast_convert_fusion
  845.9 5.0 reduce-scatter.22.cloned.1.call-done
  853.0 26.7 %reduce-scatter.14.cloned.1.call-done = bf16[192,384]{1,0:T(8,128)(2,1)} async-done(((bf16[768,384]{1,0:T(8,128)(2,1)}), bf16[192,384]{1,0:T(8,128)(2,1)}) %reduce-scatter.14.cloned.1.call-update) | async-done | bytes 147472 | tf_op jit(solution)/shard_map/reduce_scatter | solution.py:264
  879.7 40.5 %reduce-scatter.20.cloned.1.call-done = bf16[192,1536]{1,0:T(8,128)(2,1)} async-done(((bf16[768,1536]{1,0:T(8,128)(2,1)}), bf16[192,1536]{1,0:T(8,128)(2,1)}) %reduce-scatter.20.cloned.1.call-update) | async-done | bytes 589840 | tf_op jit(solution)/shard_map/reduce_scatter | solution.py:273
  920.1 40.3 %reduce-scatter.16.cloned.1.call-done = bf16[192,1536]{1,0:T(8,128)(2,1)} async-done(((bf16[768,1536]{1,0:T(8,128)(2,1)}), bf16[192,1536]{1,0:T(8,128)(2,1)}) %reduce-scatter.16.cloned.1.call-update) | async-done | bytes 589840 | tf_op jit(solution)/shard_map/reduce_scatter | solution.py:267
  960.4 40.3 %reduce-scatter.18.cloned.1.call-done = bf16[192,1536]{1,0:T(8,128)(2,1)} async-done(((bf16[768,1536]{1,0:T(8,128)(2,1)}), bf16[192,1536]{1,0:T(8,128)(2,1)}) %reduce-scatter.18.cloned.1.call-update) | async-done | bytes 589840 | tf_op jit(solution)/shard_map/reduce_scatter | solution.py:270
  1003.4 15.1 %all-reduce.10 = (bf16[768]{0:T(1024)(128)(2,1)S(1)}, bf16[768]{0:T(1024)(128)(2,1)S(1)}, bf16[768]{0:T(1024)(128)(2,1)S(1)}, bf16[768]{0:T(1024)(128)(2,1)S(1)}, bf16[768]{0:T(1024)(128)(2,1)S(1)}) all-reduce(bf16[768]{0:T(1024)(128)(2,1)S(1)} %dynamic-update-slice.3, ...), channel_id=1, replica_groups=mesh['dp'=4,'ctx'=4,'tp'=2] {'dp'}, use_global_device_ids=true, to_apply=%add.3 | all-reduce | flops 3840 | bytes 15360
  1018.7 11.7 %all-reduce.8 = (bf16[192]{0:T(256)(128)(2,1)S(1)}, bf16[192]{0:T(256)(128)(2,1)S(1)}, bf16[192]{0:T(256)(128)(2,1)S(1)}, bf16[192]{0:T(256)(128)(2,1)S(1)}) all-reduce(bf16[192]{0:T(256)(128)(2,1)S(1)} %dynamic-slice.5, bf16[192]{0:T(256)(128)(2,1)S(1)} %dynamic-slice.7, ...), channel_id=1, replica_groups=mesh['dp'=4,'ctx'=4,'tp'=2] {'ctx'}, use_global_device_ids=true, to_apply=%region_33.34 | all-reduce | flops 768 | bytes 3072 | tf_op jit(solution)/shard_map/psum | solution.py:295
  1038.2 90.7 %all-reduce.26.cloned.1.call-done = (bf16[192,3,384]{0,2,1:T(8,128)(2,1)}, bf16[192,384]{1,0:T(8,128)(2,1)}, bf16[192,1536]{1,0:T(8,128)(2,1)}, bf16[192,1536]{1,0:T(8,128)(2,1)}, bf16[192,1536]{1,0:T(8,128)(2,1)}) async-done(((bf16[192,3,384]{0,2,1:T(8,128)(2,1)}, bf16[192,384]{1,0:T(8,128)(2,1)}, bf16[192,1536]{1,0:T(8,128)(2,1)}, bf16[192,1536]{1,0:T(8,128)(2,1)}, bf16[192,1536]{1,0:T(8,128)(2,1)}), ...) | async-done | bytes 2359312 | tf_op jit(solution)/shard_map/psum | solution.py:290
  (296 shorter events, 146.1 us)
Async XLA Ops:
  7.2 40.5 %copy-start.6 = (bf16[2,512,768]{2,1,0:T(8,128)(2,1)S(1)}, bf16[2,512,768]{2,1,0:T(8,128)(2,1)}, u32[]{:S(2)}) copy-start(bf16[2,512,768]{2,1,0:T(8,128)(2,1)} %param.16) | copy-start | bytes 4718596
  7.2 37.9 %all-gather.6.cloned.1.call-start = ((), (), s32[]{:S(2)}) async-start(), calls=%async_computation.7 | async-start | bytes 2211840 | tf_op jit(solution)/shard_map/all_gather | solution.py:99
  7.9 207.7 %all-gather.8.cloned.1.call-start = ((), (), s32[]{:S(2)}) async-start(), calls=%async_computation.8 | async-start | bytes 3932160 | tf_op jit(solution)/shard_map/all_gather | solution.py:135
  52.9 259.4 %all-reduce.18.cloned.1.call-start = ((), (), s32[]{:S(2)}) async-start(), calls=%async_computation.9 | async-start | bytes 3145728 | tf_op jit(solution)/shard_map/psum | solution.py:154
  58.5 65.0 %copy-start.37 = (s32[2,512]{1,0:T(2,128)S(1)}, s32[2,512]{1,0:T(2,128)}, u32[]{:S(2)}) copy-start(s32[2,512]{1,0:T(2,128)} %param.17) | copy-start | bytes 12292
  58.5 141.1 %copy-start.38 = (bf16[192,384]{1,0:T(8,128)(2,1)S(1)}, bf16[192,384]{1,0:T(8,128)(2,1)}, u32[]{:S(2)}) copy-start(bf16[192,384]{1,0:T(8,128)(2,1)} %param.20) | copy-start | bytes 442372
  59.2 60.3 %collective-permute-start = (bf16[2,512,384]{1,2,0:T(8,128)(2,1)S(1)}, bf16[2,512,384]{1,2,0:T(8,128)(2,1)S(1)}, u32[]{:S(2)}, u32[]{:S(2)}) collective-permute-start(bf16[2,512,384]{1,2,0:T(8,128)(2,1)S(1)} %fusion.80), channel_id=1, source_target_pairs={{0,2},{2,0},{4,6},{6,4},{1,3},{3,1},{5,7},{7,5},{8,10},{10,8},{12,... | collective-permute-start | bytes 2359304 | tf_op jit(solution)/shard_map/ppermute | solution.py:15
  121.1 90.3 %collective-permute-start.1 = (bf16[2,1024,384]{1,2,0:T(8,128)(2,1)}, bf16[2,1024,384]{1,2,0:T(8,128)(2,1)S(1)}, u32[]{:S(2)}, u32[]{:S(2)}) collective-permute-start(bf16[2,1024,384]{1,2,0:T(8,128)(2,1)} %maximum_select_fusion.2), channel_id=1, source_target_pairs={{0,4},{2,6},{4,0},{6,2},{1,5},{3,7},{5,1},{7,3},{8,12},{10,14},{12... | collective-permute-start | bytes 4718600 | tf_op jit(solution)/shard_map/ppermute | solution.py:15
  228.0 12.1 %copy-start.17 = (bf16[2,2048,6,64]{1,3,2,0:T(8,128)(2,1)S(1)}, bf16[2,2048,6,64]{1,3,2,0:T(8,128)(2,1)}, u32[]{:S(2)}) copy-start(bf16[2,2048,6,64]{1,3,2,0:T(8,128)(2,1)} %get-tuple-element.428) | copy-start | bytes 9437188 | tf_op jit(solution)/shard_map/while
  264.9 12.1 %copy-start.17 = (bf16[2,2048,6,64]{1,3,2,0:T(8,128)(2,1)S(1)}, bf16[2,2048,6,64]{1,3,2,0:T(8,128)(2,1)}, u32[]{:S(2)}) copy-start(bf16[2,2048,6,64]{1,3,2,0:T(8,128)(2,1)} %get-tuple-element.428) | copy-start | bytes 9437188 | tf_op jit(solution)/shard_map/while
  294.6 58.0 %all-gather.10.cloned.1.call-start = ((), (), s32[]{:S(2)}) async-start(), calls=%async_computation.10 | async-start | bytes 2949120 | tf_op jit(solution)/shard_map/all_gather | solution.py:101
  295.1 96.5 %all-gather.12.cloned.1.call-start = ((), (), s32[]{:S(2)}) async-start(), calls=%async_computation.11 | async-start | bytes 2949120 | tf_op jit(solution)/shard_map/all_gather | solution.py:102
  295.7 135.0 %all-gather.14.cloned.1.call-start = ((), (), s32[]{:S(2)}) async-start(), calls=%async_computation.12 | async-start | bytes 2949120 | tf_op jit(solution)/shard_map/all_gather | solution.py:103
  296.3 161.3 %all-reduce.20.cloned.1.call-start = ((), (), s32[]{:S(2)}) async-start(), calls=%async_computation.13 | async-start | bytes 3145728 | tf_op jit(solution)/shard_map/psum | solution.py:166
  437.1 65.9 %all-reduce.22.cloned.1.call-start = ((), (), s32[]{:S(2)}) async-start(), calls=%async_computation.14 | async-start | bytes 3145728 | tf_op jit(solution)/shard_map/psum | solution.py:203
  437.6 27.9 %copy-start.39 = (f32[768]{0:T(1024)}, f32[768]{0:T(1024)S(1)}, u32[]{:S(2)}) copy-start(f32[768]{0:T(1024)S(1)} %convert_element_type.220) | copy-start | bytes 9220
  466.8 7.4 copy-start.14
  467.3 6.9 copy-start.49
  481.3 263.4 %reduce-scatter.10.cloned.1.call-start = ((), (), s32[]{:S(2)}) async-start(), calls=%async_computation.15 | async-start | bytes 3932160 | tf_op jit(solution)/shard_map/reduce_scatter | solution.py:239
  524.0 26.5 %copy-start = (pred[512,2048]{1,0:T(8,128)(4,1)}, pred[512,2048]{1,0:T(8,128)(4,1)S(1)}, u32[]{:S(2)}) copy-start(pred[512,2048]{1,0:T(8,128)(4,1)S(1)} %broadcast_compare_fusion.5) | copy-start | bytes 3145732 | tf_op jit(solution)/shard_map/while
  524.0 13.7 %copy-start.19 = (bf16[2,512,6,64]{1,3,2,0:T(8,128)(2,1)S(1)}, bf16[2,512,6,64]{1,3,2,0:T(8,128)(2,1)}, u32[]{:S(2)}) copy-start(bf16[2,512,6,64]{1,3,2,0:T(8,128)(2,1)} %get-tuple-element.467) | copy-start | bytes 2359300 | tf_op jit(solution)/shard_map/while
  570.5 17.8 %copy-start.5 = (bf16[2,512,6,64]{1,3,2,0:T(8,128)(2,1)S(1)}, bf16[2,512,6,64]{1,3,2,0:T(8,128)(2,1)}, u32[]{:S(2)}) copy-start(bf16[2,512,6,64]{1,3,2,0:T(8,128)(2,1)} %get-tuple-element.465) | copy-start | bytes 2359300 | tf_op jit(solution)/shard_map/while
  604.5 26.5 %copy-start = (pred[512,2048]{1,0:T(8,128)(4,1)}, pred[512,2048]{1,0:T(8,128)(4,1)S(1)}, u32[]{:S(2)}) copy-start(pred[512,2048]{1,0:T(8,128)(4,1)S(1)} %broadcast_compare_fusion.5) | copy-start | bytes 3145732 | tf_op jit(solution)/shard_map/while
  604.5 13.7 %copy-start.19 = (bf16[2,512,6,64]{1,3,2,0:T(8,128)(2,1)S(1)}, bf16[2,512,6,64]{1,3,2,0:T(8,128)(2,1)}, u32[]{:S(2)}) copy-start(bf16[2,512,6,64]{1,3,2,0:T(8,128)(2,1)} %get-tuple-element.467) | copy-start | bytes 2359300 | tf_op jit(solution)/shard_map/while
  651.0 17.8 %copy-start.5 = (bf16[2,512,6,64]{1,3,2,0:T(8,128)(2,1)S(1)}, bf16[2,512,6,64]{1,3,2,0:T(8,128)(2,1)}, u32[]{:S(2)}) copy-start(bf16[2,512,6,64]{1,3,2,0:T(8,128)(2,1)} %get-tuple-element.465) | copy-start | bytes 2359300 | tf_op jit(solution)/shard_map/while
  683.0 124.3 %reduce-scatter.12.cloned.1.call-start = ((), (), s32[]{:S(2)}) async-start(), calls=%async_computation.16 | async-start | bytes 3932160 | tf_op jit(solution)/shard_map/reduce_scatter | solution.py:242
  683.6 167.3 %reduce-scatter.22.cloned.1.call-start = ((), (), s32[]{:S(2)}) async-start(), calls=%async_computation.22 | async-start | bytes 2211840
  685.7 60.4 %copy-start.22 = (f32[2,512,6,64]{1,3,2,0:T(8,128)S(1)}, f32[2,512,6,64]{1,3,2,0:T(8,128)}, u32[]{:S(2)}) copy-start(f32[2,512,6,64]{1,3,2,0:T(8,128)} %get-tuple-element.115) | copy-start | bytes 4718596
  685.7 60.4 %copy-start.30 = (f32[512,64]{0,1:T(8,128)S(1)}, f32[512,64]{0,1:T(8,128)}, u32[]{:S(2)}) copy-start(f32[512,64]{0,1:T(8,128)} %copy-done.29) | copy-start | bytes 393220
  756.1 53.6 %copy-start.9 = (bf16[2,512,768]{2,1,0:T(8,128)(2,1)S(1)}, bf16[2,512,768]{2,1,0:T(8,128)(2,1)}, u32[]{:S(2)}) copy-start(bf16[2,512,768]{2,1,0:T(8,128)(2,1)} %param.16) | copy-start | bytes 4718596
  818.4 61.3 %reduce-scatter.14.cloned.1.call-start = ((), (), s32[]{:S(2)}) async-start(), calls=%async_computation.18 | async-start | bytes 737280 | tf_op jit(solution)/shard_map/reduce_scatter | solution.py:264
  821.6 7.1 copy-start.32
  821.6 98.5 %reduce-scatter.20.cloned.1.call-start = ((), (), s32[]{:S(2)}) async-start(), calls=%async_computation.21 | async-start | bytes 2949120 | tf_op jit(solution)/shard_map/reduce_scatter | solution.py:273
  828.7 131.7 %reduce-scatter.16.cloned.1.call-start = ((), (), s32[]{:S(2)}) async-start(), calls=%async_computation.19 | async-start | bytes 2949120 | tf_op jit(solution)/shard_map/reduce_scatter | solution.py:267
  834.7 6.1 copy-start.31
  834.7 166.0 %reduce-scatter.18.cloned.1.call-start = ((), (), s32[]{:S(2)}) async-start(), calls=%async_computation.20 | async-start | bytes 2949120 | tf_op jit(solution)/shard_map/reduce_scatter | solution.py:270
  840.7 193.7 %all-reduce.24.cloned.1.call-start = ((), (), s32[]{:S(2)}) async-start(), calls=%async_computation.17 | async-start | bytes 3145728 | tf_op jit(solution)/shard_map/psum | solution.py:256
  845.8 157.3 %copy-start.55 = (bf16[192]{0:T(256)(128)(2,1)S(1)}, bf16[192]{0:T(256)(128)(2,1)}, u32[]{:S(2)}) copy-start(bf16[192]{0:T(256)(128)(2,1)} %param.27) | copy-start | bytes 1156
  845.8 157.6 %copy-start.45 = (bf16[768]{0:T(1024)(128)(2,1)S(1)}, bf16[768]{0:T(1024)(128)(2,1)}, u32[]{:S(2)}) copy-start(bf16[768]{0:T(1024)(128)(2,1)} %get-tuple-element.186) | copy-start | bytes 4612
  845.8 157.6 %copy-start.46 = (bf16[768]{0:T(1024)(128)(2,1)S(1)}, bf16[768]{0:T(1024)(128)(2,1)}, u32[]{:S(2)}) copy-start(bf16[768]{0:T(1024)(128)(2,1)} %get-tuple-element.184) | copy-start | bytes 4612
  845.8 157.6 %copy-start.47 = (bf16[768]{0:T(1024)(128)(2,1)S(1)}, bf16[768]{0:T(1024)(128)(2,1)}, u32[]{:S(2)}) copy-start(bf16[768]{0:T(1024)(128)(2,1)} %get-tuple-element.189) | copy-start | bytes 4612
  845.8 186.9 %copy-start.4 = (f32[1024,768]{1,0:T(8,128)S(1)}, f32[1024,768]{1,0:T(8,128)}, u32[]{:S(2)}) copy-start(f32[1024,768]{1,0:T(8,128)} %copy-done.3) | copy-start | bytes 9437188
  845.8 186.9 %copy-start.40 = (f32[768]{0:T(1024)S(1)}, f32[768]{0:T(1024)}, u32[]{:S(2)}) copy-start(f32[768]{0:T(1024)} %copy-done.39) | copy-start | bytes 9220
  845.8 186.9 %copy-start.42 = (f32[1024]{0:T(1024)S(1)}, f32[1024]{0:T(1024)}, u32[]{:S(2)}) copy-start(f32[1024]{0:T(1024)} %copy-done.41) | copy-start | bytes 12292
  845.8 186.9 %copy-start.44 = (f32[1024]{0:T(1024)S(1)}, f32[1024]{0:T(1024)}, u32[]{:S(2)}) copy-start(f32[1024]{0:T(1024)} %copy-done.43) | copy-start | bytes 12292
  845.9 283.1 %all-reduce.26.cloned.1.call-start = ((), (), s32[]{:S(2)}) async-start(), calls=%async_computation.23 | async-start | bytes 5013504 | tf_op jit(solution)/shard_map/psum | solution.py:290
  1128.9 6.2 copy-start.36
  1128.9 7.3 copy-start.35
  (39 other events, 129.9 us)
Sparse Core Ops, SparseCore 0:
  9.8 35.1 all-gather.5
  53.0 82.9 all-gather.7
  294.7 17.5 all-reduce.17
  314.0 38.5 all-gather.9
  354.2 37.3 all-gather.11
  393.3 37.3 all-gather.13
  437.2 20.3 all-reduce.19
  481.5 21.5 all-reduce.21
  683.2 61.5 reduce-scatter.9
  746.9 60.3 reduce-scatter.11
  818.5 32.3 reduce-scatter.21
  854.2 25.3 reduce-scatter.13
  882.7 37.3 reduce-scatter.19
  923.0 37.3 reduce-scatter.15
  963.3 37.3 reduce-scatter.17
  1003.5 20.3 all-reduce.23
  1027.1 101.7 all-reduce.25
